TPU v7x, 256 devices: a whole 4x4x8 slice. The times are simulated.
256 devices in a mesh: seq: 64 (over y, z, core), section: 4 (over x).
Axes of the slice: x: 4, y: 4, z: 8, core: 2. Of those that a mesh axis runs over, the one named last changes fastest.
Arguments:
- acts: bfloat16 [16384, 1408], P('seq'), may hold values from -16 to 16
- pre_act: bfloat16 [16384, 1536], P('seq', 'section'), may hold values from -6 to 6
- emb_grad: bfloat16 [8192, 1536], P('seq', 'section'), may hold values from -6 to 6
- filters: bfloat16 [7040, 1536], P('seq', 'section'), may hold values from -0.0625 to 0.0625
Outputs:
- input_grad: bfloat16 [16384, 1408], P('seq', 'section')
- filter_grad: float32 [7040, 1536], P('seq', 'section')
All inputs are finite; a program needn't handle non-finite values.
Results may differ from a plain program's by a relative error of at most 0.0049.
Values may be sent and summed in bfloat16 or wider, within the bound.
A program may use at most 128 MiB of HBM per device.

v0:
```python
import math
import jax
import jax.numpy as jnp
from jax import lax
from jax.sharding import PartitionSpec as P

KERNEL = 5
SEQS = 1


def with_halo(shard, sides, width):
    for axis, dim in sides:
        size, length = (lax.axis_size(axis), shard.shape[dim])
        up = [(i, (i + 1) % size) for i in range(size - 1)]
        down = [(j, i) for i, j in up]
        last = lax.slice_in_dim(shard, length - width, length, axis=dim)
        first = lax.slice_in_dim(shard, 0, width, axis=dim)
        before = lax.ppermute(last, axis, up)
        after = lax.ppermute(first, axis, down)
        shard = jnp.concatenate([before, shard, after], axis=dim)
    return shard


def gelu_slope(value):
    cumul = 0.5 * (1.0 + lax.erf(value * 0.7071067811865476))
    dens = jnp.exp(-0.5 * value * value) * 0.3989422804014327
    return cumul + value * dens


def shards(acts, pre_act, emb_grad, filters):
    rows = acts.shape[0]
    c_in = acts.shape[1]
    upward = jnp.repeat(emb_grad.astype(jnp.float32), 2, axis=0) * 0.5
    zvalue = pre_act.astype(jnp.float32)
    dz_grad = (upward * gelu_slope(zvalue)).astype(jnp.bfloat16)
    total_rows = rows * lax.axis_size("seq")
    length = total_rows // SEQS
    first = lax.axis_index("seq") * rows
    positions = first - 2 + jnp.arange(rows + 4, dtype=jnp.int32)
    inside = (jnp.floor_divide(positions, length) == first // length).astype(jnp.bfloat16)[:, None]
    scale_value = 1.0 / math.sqrt(total_rows)
    grad_rim = with_halo(dz_grad, (("seq", 0),), 2) * inside
    whole_term = (
        jnp.concatenate(
            [
                jnp.einsum(
                    "rc,ro->co",
                    acts,
                    grad_rim[4 - k : 4 - k + rows],
                    preferred_element_type=jnp.float32,
                )
                for k in range(KERNEL)
            ],
            axis=0,
        )
        * scale_value
    )
    piece = lax.all_gather(filters, "seq", axis=0, tiled=True)
    width = piece.shape[0]
    product = jnp.einsum("ro,no->rn", grad_rim, piece, preferred_element_type=jnp.float32)
    tap_of = jnp.arange(width, dtype=jnp.int32) // c_in
    total = jnp.zeros((rows, width), jnp.float32)
    for k in range(KERNEL):
        total = total + jnp.where((tap_of == k)[None, :], product[4 - k : 4 - k + rows], 0.0)
    partial_input = total.reshape(rows, KERNEL, c_in).sum(axis=1)
    input_grad = lax.psum_scatter(partial_input, "section", scatter_dimension=1, tiled=True).astype(
        jnp.bfloat16
    )
    filter_grad = lax.psum_scatter(whole_term, "seq", scatter_dimension=0, tiled=True)
    return (input_grad, filter_grad)


def solution(mesh):
    in_specs = (P("seq", None), P("seq", "section"), P("seq", "section"), P("seq", "section"))
    out_specs = (P("seq", "section"), P("seq", "section"))
    return jax.shard_map(shards, mesh=mesh, in_specs=in_specs, out_specs=out_specs, check_vma=False)
```

profile of v0, /device:TPU:8, one launch (start us, length us, event | category | flops | bytes accessed | tf_op | source)
XLA Modules:
  0.0 342.2 jit_solution(12863627836406627910)
XLA Ops:
  7.2 0.7 all-gather.3.cloned.1.call-update
  8.0 0.9 convert_multiply_fusion.4
  9.3 1.1 fusion.16
  10.4 7.1 %collective-permute-start.1 = (bf16[2,384]{1,0:T(2,128)(2,1)S(1)}, bf16[2,384]{1,0:T(2,128)(2,1)S(1)}, u32[]{:S(2)}, u32[]{:S(2)}) collective-permute-start(bf16[2,384]{1,0:T(2,128)(2,1)S(1)} %get-tuple-element.9), channel_id=1, source_target_pairs={{4,0},{8,4},{12,8},{16,12},{20,16},{24,20},{28,24},{32,28},{36,32}... | collective-permute-start | bytes 4616 | tf_op jit(solution)/shard_map/ppermute | solution.py:19
  17.5 1.9 collective-permute-start
  19.5 5.0 %collective-permute-done = bf16[2,384]{1,0:T(2,128)(2,1)S(1)} collective-permute-done((bf16[2,384]{1,0:T(2,128)(2,1)S(1)}, bf16[2,384]{1,0:T(2,128)(2,1)S(1)}, u32[]{:S(2)}, u32[]{:S(2)}) %collective-permute-start) | collective-permute-done | bytes 1568 | tf_op jit(solution)/shard_map/ppermute | solution.py:18
  24.7 0.5 fusion.8
  25.2 0.5 fusion.7
  25.7 0.5 fusion.6
  26.2 0.5 fusion.5
  26.7 0.5 fusion.4
  27.2 4.6 %broadcast_multiply_fusion = f32[7040,384]{0,1:T(8,128)} fusion(f32[7040,384]{0,1:T(8,128)S(1)} %fusion.4), kind=kLoop, calls=%fused_computation.9 | loop fusion | flops 2703360 | bytes 21626880 | tf_op jit(solution)/shard_map/mul | solution.py:44
  32.0 60.9 %all-gather.3.cloned.1.call-done = bf16[64,110,384]{2,1,0:T(8,128)(2,1)} async-done(((bf16[1,110,384]{2,1,0:T(8,128)(2,1)}), bf16[64,110,384]{2,1,0:T(8,128)(2,1)}) %all-gather.3.cloned.1.call-update) | async-done | bytes 5406736 | tf_op jit(solution)/shard_map/all_gather | solution.py:58
  92.9 7.7 %reshape.59 = bf16[7040,384]{1,0:T(8,128)(2,1)} reshape(bf16[64,110,384]{2,1,0:T(8,128)(2,1)} %all-gather.3.cloned.1.call-done) | data formatting | bytes 10813440
  100.6 4.7 %fusion.30 = f32[260,7040]{1,0:T(8,128)S(1)} fusion(bf16[7040,384]{1,0:T(8,128)(2,1)} %reshape.59, bf16[2,384]{1,0:T(2,128)(2,1)S(1)} %collective-permute-done.1, bf16[256,384]{1,0:T(8,128)(2,1)S(1)} %fusion.16, bf16[2,384]{1,0:T(2,128)(2,1)S(1)} %collective-permute-done, bf16[260]{0:T(512)(128)(2,1)S(1)} %fusion.29), kind=kOutput, calls=%fused_computation.63 | convolution fusion | flops 1406545920 | bytes 12928520 | tf_op jit(solution)/shard_map/ro,no->rn/dot_general | solution.py:60
  105.3 6.0 %fusion = f32[256,7040]{1,0:T(8,128)} fusion(f32[260,7040]{1,0:T(8,128)S(1)} %fusion.30, pred[7040]{0:T(1024)(128)(4,1)S(1)} %get-tuple-element.10, pred[7040]{0:T(1024)(128)(4,1)S(1)} %get-tuple-element.11, pred[7040]{0:T(1024)(128)(4,1)S(1)} %get-tuple-element.12, pred[7040]{0:T(1024)(128)(4,1)S(1)} %broadcast_compare_fusion.4, ...), kind=kLoop, calls=%fused_computation.1 | loop fusion | flops 16220160 | bytes 43288960 | tf_op jit(solution)/shard_map/add | solution.py:64
  111.3 8.8 %copy.9 = f32[256,7040]{0,1:T(8,128)} copy(f32[256,7040]{1,0:T(8,128)} %fusion) | data formatting | bytes 14417920 | tf_op jit(solution)/shard_map/add | solution.py:64
  120.1 4.9 %reduce_sum.9 = f32[256,1408]{0,1:T(8,128)} reduce(f32[256,5,1408]{0,2,1:T(8,128)} %bitcast.31, f32[]{:T(128)} %constant.61.clone.1), dimensions={1}, to_apply=%region_0.1 | reduce | flops 1441792 | bytes 8650756 | tf_op jit(solution)/shard_map/reduce_sum | solution.py:65
  125.1 0.6 dynamic-slice
  126.3 178.5 %all-reduce.3.cloned.1.call-done = f32[7040,384]{0,1:T(8,128)} async-done(((f32[7040,384]{0,1:T(8,128)}), f32[7040,384]{0,1:T(8,128)}) %all-reduce.3.cloned.1.call-update) | async-done | bytes 10813456
  304.9 1.1 constant_dynamic-slice_fusion
  306.0 0.8 copy.10
  306.8 27.2 %reduce-scatter.3.cloned.1.call-done = f32[256,352]{0,1:T(8,128)} async-done(((f32[256,1408]{0,1:T(8,128)}), f32[256,352]{0,1:T(8,128)}) %reduce-scatter.3.cloned.1.call-update) | async-done | bytes 360464 | tf_op jit(solution)/shard_map/reduce_scatter | solution.py:66
  334.0 1.7 convert_element_type.23
  (20 shorter events, 0.8 us)
Async XLA Ops:
  7.2 17.5 %copy-start = (bf16[256,1408]{1,0:T(8,128)(2,1)S(1)}, bf16[256,1408]{1,0:T(8,128)(2,1)}, u32[]{:S(2)}) copy-start(bf16[256,1408]{1,0:T(8,128)(2,1)} %param.4) | copy-start | bytes 2162692
  7.2 85.7 %all-gather.3.cloned.1.call-start = ((), (), s32[]{:S(2)}) async-start(), calls=%async_computation.2 | async-start | bytes 5591040 | tf_op jit(solution)/shard_map/all_gather | solution.py:58
  7.9 297.0 %all-reduce.3.cloned.1.call-start = ((), (), s32[]{:S(2)}) async-start(), calls=%async_computation.3 | async-start | bytes 21626880
  10.4 9.1 %collective-permute-start.1 = (bf16[2,384]{1,0:T(2,128)(2,1)S(1)}, bf16[2,384]{1,0:T(2,128)(2,1)S(1)}, u32[]{:S(2)}, u32[]{:S(2)}) collective-permute-start(bf16[2,384]{1,0:T(2,128)(2,1)S(1)} %get-tuple-element.9), channel_id=1, source_target_pairs={{4,0},{8,4},{12,8},{16,12},{20,16},{24,20},{28,24},{32,28},{36,32}... | collective-permute-start | bytes 4616 | tf_op jit(solution)/shard_map/ppermute | solution.py:19
  17.5 7.0 %collective-permute-start = (bf16[2,384]{1,0:T(2,128)(2,1)S(1)}, bf16[2,384]{1,0:T(2,128)(2,1)S(1)}, u32[]{:S(2)}, u32[]{:S(2)}) collective-permute-start(bf16[2,384]{1,0:T(2,128)(2,1)S(1)} %get-tuple-element.8), channel_id=1, source_target_pairs={{0,4},{4,8},{8,12},{12,16},{16,20},{20,24},{24,28},{28,32},{32,36}... | collective-permute-start | bytes 4616 | tf_op jit(solution)/shard_map/ppermute | solution.py:18
  31.8 302.2 %reduce-scatter.3.cloned.1.call-start = ((), (), s32[]{:S(2)}) async-start(), calls=%async_computation.1 | async-start | bytes 1802240 | tf_op jit(solution)/shard_map/reduce_scatter | solution.py:66
  111.3 224.4 %copy-start.1 = (bf16[256,1408]{1,0:T(8,128)(2,1)S(1)}, bf16[256,1408]{1,0:T(8,128)(2,1)}, u32[]{:S(2)}) copy-start(bf16[256,1408]{1,0:T(8,128)(2,1)} %param.4) | copy-start | bytes 2162692
  120.1 5.0 %copy-start.2 = (u32[256]{0:T(256)S(1)}, u32[256]{0:T(256)}, u32[]{:S(2)}) copy-start(u32[256]{0:T(256)} %constant.69) | copy-start | bytes 3076
Sparse Core Ops, SparseCore 0:
  10.7 82.1 all-gather.2
  96.5 208.2 all-reduce.2
  307.6 26.3 reduce-scatter.2
where the time goes:
time: 343 us; the launch traced here: 342 us
  waiting for transfers between devices  272 us (79%)
  local copies, waits for them, and re-layouts  19.5 us (6%)
  other arithmetic  19.4 us (6%)
  between operations  14.6 us (4%)
  starting transfers between devices  9.13 us (3%)
  matrix products  7.19 us (2%)
    unnamed x4, waiting for transfers between devices  179 us
    all_gather x1, waiting for transfers between devices, shards(): piece = lax.all_gather(filters, 'seq', axis=0, tiled=True)  60.9 us
    reduce_scatter x1, waiting for transfers between devices, shards(): lax.psum_scatter(partial_input, 'section', scatter_dimension=1, tiled=True)  27.2 us
    unnamed x10, local copies, waits for them, and re-layouts  10.3 us
    add x1, local copies, waits for them, and re-layouts, shards(): total + jnp.where((tap_of == k)[None, :], product[4 - k:4 - k + rows], 0.0)  8.77 us
    ppermute x1, starting transfers between devices, with_halo(): after = lax.ppermute(first, axis, down)  7.09 us
  transfers between devices with their start and end apart: 5, of which 4 were waited for; matrix products, arithmetic and copies ran while one was open for 13% of the time, Pallas kernels for 0%

commit v1 on v0

--- a/solution.py
+++ b/solution.py
@@ -6,6 +6,11 @@
 
 KERNEL = 5
 SEQS = 1
+
+
+def all_by_exchange(x, name, dim):
+    sent = jnp.stack([x] * lax.axis_size(name))
+    return jnp.concatenate(lax.all_to_all(sent, name, 0, 0), axis=dim)
 
 
 def with_halo(shard, sides, width):
@@ -55,7 +60,7 @@
         )
         * scale_value
     )
-    piece = lax.all_gather(filters, "seq", axis=0, tiled=True)
+    piece = all_by_exchange(filters, "seq", 0)
     width = piece.shape[0]
     product = jnp.einsum("ro,no->rn", grad_rim, piece, preferred_element_type=jnp.float32)
     tap_of = jnp.arange(width, dtype=jnp.int32) // c_in

time: 343 us -> 374 us (1.090)
  waiting for transfers between devices: 272 us -> 290 us
  starting transfers between devices: 9.13 us -> 18.7 us
  local copies, waits for them, and re-layouts: 19.5 us -> 23.4 us
    ppermute x1, waiting for transfers between devices: 0.01 us -> 109 us  [with_halo(): after = lax.ppermute(first, axis, down)]
    all_gather x1 -> x0, waiting for transfers between devices: 60.9 us -> none  [shards(): piece = lax.all_gather(filters, 'seq', axis=0, tiled=True)]
    reduce_scatter x1, waiting for transfers between devices: 27.2 us -> 0.01 us  [shards(): lax.psum_scatter(partial_input, 'section', scatter_dimension=1, tiled=True)]
    all_to_all x0 -> x1, starting transfers between devices: none -> 12.4 us  [all_by_exchange(): return jnp.concatenate(lax.all_to_all(sent, name, 0, 0), axis=dim)]
    reshape x0 -> x1, local copies, waits for them, and re-layouts: none -> 7.77 us  [all_by_exchange(): return jnp.concatenate(lax.all_to_all(sent, name, 0, 0), axis=dim)]
    unnamed x10 -> x13, local copies, waits for them, and re-layouts: 10.3 us -> 2.53 us
    another operation x0 -> x1, local copies, waits for them, and re-layouts: none -> 3.9 us  [all_by_exchange(): sent = jnp.stack([x] * lax.axis_size(name))]
    unnamed x4 -> x3, waiting for transfers between devices: 179 us -> 179 us
  transfers between devices with their start and end apart: 5 -> 5, of which waited for: 4 -> 3; matrix products, arithmetic and copies ran while one was open for 13% -> 11% of each run, Pallas kernels for 0% -> 0%
where the time goes in v1:
time: 374 us; the launch traced here: 373 us
  waiting for transfers between devices  290 us (78%)
  local copies, waits for them, and re-layouts  23.4 us (6%)
  starting transfers between devices  18.7 us (5%)
  other arithmetic  17.6 us (5%)
  between operations  16.3 us (4%)
  matrix products  7.19 us (2%)
    unnamed x3, waiting for transfers between devices  179 us
    ppermute x1, waiting for transfers between devices, with_halo(): after = lax.ppermute(first, axis, down)  109 us
    all_to_all x1, starting transfers between devices, all_by_exchange(): return jnp.concatenate(lax.all_to_all(sent, name, 0, 0), axis=dim)  12.4 us
    add x1, local copies, waits for them, and re-layouts, shards(): total + jnp.where((tap_of == k)[None, :], product[4 - k:4 - k + rows], 0.0)  8.76 us
    reshape x1, local copies, waits for them, and re-layouts, all_by_exchange(): return jnp.concatenate(lax.all_to_all(sent, name, 0, 0), axis=dim)  7.77 us
  transfers between devices with their start and end apart: 5, of which 3 were waited for; matrix products, arithmetic and copies ran while one was open for 11% of the time, Pallas kernels for 0%

profile of v1, /device:TPU:8, one launch (start us, length us, event | category | flops | bytes accessed | tf_op | source)
XLA Modules:
  0.0 373.3 jit_solution(4896163097983277382)
XLA Ops:
  8.0 3.9 %stack.2 = bf16[64,110,384]{2,1,0:T(8,128)(2,1)} broadcast(bf16[110,384]{1,0:T(8,128)(2,1)} %param.7), dimensions={1,2} | broadcast | bytes 5491200 | tf_op jit(solution)/shard_map/stack | solution.py:12
  11.9 12.4 %all-to-all-start = ((bf16[64,110,384]{2,1,0:T(8,128)(2,1)}), bf16[64,110,384]{2,1,0:T(8,128)(2,1)}, u32[]{:S(2)}, u32[]{:S(2)}) async-start(bf16[64,110,384]{2,1,0:T(8,128)(2,1)} %stack.2), calls=%async_computation | async-start | bytes 11010048 | tf_op jit(solution)/shard_map/all_to_all | solution.py:13
  24.6 0.3 mul.55
  24.9 0.2 fusion.16
  25.1 4.3 %collective-permute-start.1 = (bf16[2,384]{1,0:T(2,128)(2,1)S(1)}, bf16[2,384]{1,0:T(2,128)(2,1)S(1)}, u32[]{:S(2)}, u32[]{:S(2)}) collective-permute-start(bf16[2,384]{1,0:T(2,128)(2,1)S(1)} %get-tuple-element.9), channel_id=1, source_target_pairs={{4,0},{8,4},{12,8},{16,12},{20,16},{24,20},{28,24},{32,28},{36,32}... | collective-permute-start | bytes 4616 | tf_op jit(solution)/shard_map/ppermute | solution.py:24
  29.4 1.9 collective-permute-start
  31.4 109.3 %collective-permute-done.1 = bf16[2,384]{1,0:T(2,128)(2,1)S(1)} collective-permute-done((bf16[2,384]{1,0:T(2,128)(2,1)S(1)}, bf16[2,384]{1,0:T(2,128)(2,1)S(1)}, u32[]{:S(2)}, u32[]{:S(2)}) %collective-permute-start.1) | collective-permute-done | bytes 1568 | tf_op jit(solution)/shard_map/ppermute | solution.py:24
  140.7 2.0 collective-permute-done
  142.8 0.5 fusion.8
  143.3 0.5 fusion.7
  143.8 0.5 fusion.6
  144.3 0.5 fusion.5
  144.8 0.5 fusion.4
  145.3 4.6 %broadcast_multiply_fusion = f32[7040,384]{0,1:T(8,128)} fusion(f32[7040,384]{0,1:T(8,128)S(1)} %fusion.4), kind=kLoop, calls=%fused_computation.9 | loop fusion | flops 2703360 | bytes 21626880 | tf_op jit(solution)/shard_map/mul | solution.py:49
  150.1 7.8 %reshape.62 = bf16[7040,384]{1,0:T(8,128)(2,1)} reshape(bf16[64,110,384]{2,1,0:T(8,128)(2,1)} %all-to-all-done) | data formatting | bytes 10813440 | tf_op jit(solution)/shard_map/reshape | solution.py:13
  157.9 4.7 %fusion.30 = f32[260,7040]{1,0:T(8,128)S(1)} fusion(bf16[7040,384]{1,0:T(8,128)(2,1)} %reshape.62, bf16[2,384]{1,0:T(2,128)(2,1)S(1)} %collective-permute-done.1, bf16[256,384]{1,0:T(8,128)(2,1)S(1)} %fusion.16, bf16[2,384]{1,0:T(2,128)(2,1)S(1)} %collective-permute-done, bf16[260]{0:T(512)(128)(2,1)S(1)} %fusion.29), kind=kOutput, calls=%fused_computation.63 | convolution fusion | flops 1406545920 | bytes 12928520 | tf_op jit(solution)/shard_map/ro,no->rn/dot_general | solution.py:65
  162.6 6.0 %fusion = f32[256,7040]{1,0:T(8,128)} fusion(f32[260,7040]{1,0:T(8,128)S(1)} %fusion.30, pred[7040]{0:T(1024)(128)(4,1)S(1)} %get-tuple-element.10, pred[7040]{0:T(1024)(128)(4,1)S(1)} %get-tuple-element.11, pred[7040]{0:T(1024)(128)(4,1)S(1)} %get-tuple-element.12, pred[7040]{0:T(1024)(128)(4,1)S(1)} %broadcast_compare_fusion.4, ...), kind=kLoop, calls=%fused_computation.1 | loop fusion | flops 16220160 | bytes 43288960 | tf_op jit(solution)/shard_map/add | solution.py:69
  168.6 8.8 %copy.9 = f32[256,7040]{0,1:T(8,128)} copy(f32[256,7040]{1,0:T(8,128)} %fusion) | data formatting | bytes 14417920 | tf_op jit(solution)/shard_map/add | solution.py:69
  177.3 4.9 %reduce_sum.9 = f32[256,1408]{0,1:T(8,128)} reduce(f32[256,5,1408]{0,2,1:T(8,128)} %bitcast.30, f32[]{:T(128)} %constant.61.clone.1), dimensions={1}, to_apply=%region_0.1 | reduce | flops 1441792 | bytes 8650756 | tf_op jit(solution)/shard_map/reduce_sum | solution.py:70
  182.3 0.6 dynamic-slice
  183.5 178.7 %all-reduce.3.cloned.1.call-done = f32[7040,384]{0,1:T(8,128)} async-done(((f32[7040,384]{0,1:T(8,128)}), f32[7040,384]{0,1:T(8,128)}) %all-reduce.3.cloned.1.call-update) | async-done | bytes 10813456
  362.3 1.1 constant_dynamic-slice_fusion
  363.4 0.8 copy.10
  364.2 1.7 convert_element_type.23
  (24 shorter events, 0.5 us)
Async XLA Ops:
  8.0 134.8 %copy-start = (bf16[256,1408]{1,0:T(8,128)(2,1)S(1)}, bf16[256,1408]{1,0:T(8,128)(2,1)}, u32[]{:S(2)}) copy-start(bf16[256,1408]{1,0:T(8,128)(2,1)} %param.4) | copy-start | bytes 2162692
  8.0 16.4 %copy-start.3 = (bf16[128,384]{1,0:T(8,128)(2,1)S(1)}, bf16[128,384]{1,0:T(8,128)(2,1)}, u32[]{:S(2)}) copy-start(bf16[128,384]{1,0:T(8,128)(2,1)} %param.6) | copy-start | bytes 294916
  11.9 12.9 %copy-start.2 = (bf16[256,384]{1,0:T(8,128)(2,1)S(1)}, bf16[256,384]{1,0:T(8,128)(2,1)}, u32[]{:S(2)}) copy-start(bf16[256,384]{1,0:T(8,128)(2,1)} %param.5) | copy-start | bytes 589828
  11.9 138.2 %all-to-all-start = ((bf16[64,110,384]{2,1,0:T(8,128)(2,1)}), bf16[64,110,384]{2,1,0:T(8,128)(2,1)}, u32[]{:S(2)}, u32[]{:S(2)}) async-start(bf16[64,110,384]{2,1,0:T(8,128)(2,1)} %stack.2), calls=%async_computation | async-start | bytes 11010048 | tf_op jit(solution)/shard_map/all_to_all | solution.py:13
  24.3 337.9 %all-reduce.3.cloned.1.call-start = ((), (), s32[]{:S(2)}) async-start(), calls=%async_computation.3 | async-start | bytes 21626880
  25.1 115.6 %collective-permute-start.1 = (bf16[2,384]{1,0:T(2,128)(2,1)S(1)}, bf16[2,384]{1,0:T(2,128)(2,1)S(1)}, u32[]{:S(2)}, u32[]{:S(2)}) collective-permute-start(bf16[2,384]{1,0:T(2,128)(2,1)S(1)} %get-tuple-element.9), channel_id=1, source_target_pairs={{4,0},{8,4},{12,8},{16,12},{20,16},{24,20},{28,24},{32,28},{36,32}... | collective-permute-start | bytes 4616 | tf_op jit(solution)/shard_map/ppermute | solution.py:24
  29.4 113.3 %collective-permute-start = (bf16[2,384]{1,0:T(2,128)(2,1)S(1)}, bf16[2,384]{1,0:T(2,128)(2,1)S(1)}, u32[]{:S(2)}, u32[]{:S(2)}) collective-permute-start(bf16[2,384]{1,0:T(2,128)(2,1)S(1)} %get-tuple-element.8), channel_id=1, source_target_pairs={{0,4},{4,8},{8,12},{12,16},{16,20},{20,24},{24,28},{28,32},{32,36}... | collective-permute-start | bytes 4616 | tf_op jit(solution)/shard_map/ppermute | solution.py:23
  150.0 214.3 %reduce-scatter.3.cloned.1.call-start = ((), (), s32[]{:S(2)}) async-start(), calls=%async_computation.2 | async-start | bytes 1802240 | tf_op jit(solution)/shard_map/reduce_scatter | solution.py:71
  168.6 197.3 %copy-start.1 = (bf16[256,1408]{1,0:T(8,128)(2,1)S(1)}, bf16[256,1408]{1,0:T(8,128)(2,1)}, u32[]{:S(2)}) copy-start(bf16[256,1408]{1,0:T(8,128)(2,1)} %param.4) | copy-start | bytes 2162692
  177.3 5.0 %copy-start.4 = (u32[256]{0:T(256)S(1)}, u32[256]{0:T(256)}, u32[]{:S(2)}) copy-start(u32[256]{0:T(256)} %constant.69) | copy-start | bytes 3076
Sparse Core Ops, SparseCore 0:
  150.1 212.1 all-reduce.2
Sparse Core Ops, SparseCore 1:
  182.4 29.2 reduce-scatter.2
